TPU v7x, 128 devices: a whole 4x4x4 slice. The times are simulated.
128 devices in a mesh: row: 8 (over z, core), col: 8 (over y_hi, x), freq: 2 (over y_lo).
Axes of the slice: x: 4, y: 4 (y_hi: 2, y_lo: 2; y = y_hi * 2 + y_lo), z: 4, core: 2. Of those that a mesh axis runs over, the one named last changes fastest.
Arguments:
- pair_elements: bfloat16 [2, 1024, 8192], P(None, ('row', 'freq'), 'col'), may hold values from -1.59375 to 1.59375
- transitions: int32 [3, 1024], replicated, may hold values from 0 to 63, as said below
- energies: float32 [16, 64], replicated, may hold values from -3 to 3
- occupations: int32 [16, 64], replicated, may hold values from 0 to 2
- frequencies: float32 [4], P('freq'), may hold values from 0.2 to 2
Outputs:
- chi_zero: float32 [4, 2, 8192, 8192], P('freq', None, 'row', 'col')
Inputs may be any that keep to these rules, and one draw needn't show every extreme that they name: transitions[0] is a k-point below 16, transitions[1] a valence band below 32, transitions[2] a conduction band of 32 to 63.
All inputs are finite; a program needn't handle non-finite values.
Results may differ from a plain program's by a relative error of at most 0.0028.
Values may be sent and summed in bfloat16 or wider, within the bound.
A program may use at most 128 MiB of HBM per device.

v0:
```python
import jax
import jax.numpy as jnp
from jax import lax
from jax.sharding import PartitionSpec as P


def broadcast(value, axis, source):
    kept = jnp.where(lax.axis_index(axis) == source, value, 0).astype(value.dtype)
    return lax.psum(kept, axis)


def lookup(table, flat_rows):
    flat = table.reshape(-1)
    onehot = (flat_rows[:, None] == jnp.arange(flat.shape[0], dtype=jnp.int32)[None, :]).astype(
        jnp.float32
    )
    return jnp.dot(onehot, flat, precision=lax.Precision.HIGHEST)


def weights(transitions, energies, occupations, frequencies):
    bands = energies.shape[1]
    kpoint = transitions[0]
    valence_rows = kpoint * bands + transitions[1]
    conduction_rows = kpoint * bands + transitions[2]
    gap = lookup(energies, conduction_rows) - lookup(energies, valence_rows)
    occ_float = occupations.astype(jnp.float32)
    filled = lookup(occ_float, valence_rows) - lookup(occ_float, conduction_rows)
    return (
        filled[None, :]
        * 2.0
        * gap[None, :]
        / (gap[None, :] * gap[None, :] + frequencies[:, None] * frequencies[:, None])
    )


def contribute(left, right, weight_block):
    right_both = jnp.concatenate([right[0], right[1]], 0)
    dims = (((0,), (0,)), ((), ()))
    results = []
    for index in range(weight_block.shape[0]):
        scaled = (left.astype(jnp.float32) * weight_block[index][None, :, None]).astype(
            jnp.bfloat16
        )
        real_left = jnp.concatenate([scaled[0], scaled[1]], 0)
        imag_left = jnp.concatenate([scaled[1], -scaled[0]], 0)
        real_component = lax.dot_general(
            real_left, right_both, dims, preferred_element_type=jnp.float32
        )
        imag_part = lax.dot_general(imag_left, right_both, dims, preferred_element_type=jnp.float32)
        results.append(jnp.stack([real_component, imag_part], 0))
    return jnp.stack(results, 0)


def body(pair_elements, transitions, energies, occupations, frequencies):
    weight = weights(transitions, energies, occupations, frequencies)
    column_panel = lax.all_gather(pair_elements, ("row", "freq"), axis=1, tiled=True)
    row_panel = broadcast(column_panel, "col", lax.axis_index("row"))
    chi_zero = contribute(row_panel, column_panel, weight)
    return chi_zero


def solution(mesh):
    in_specs = (P(None, ("row", "freq"), "col"), P(), P(), P(), P("freq"))
    out_specs = P("freq", None, "row", "col")
    return jax.shard_map(body, mesh=mesh, in_specs=in_specs, out_specs=out_specs, check_vma=False)
```

profile of v0, /device:TPU:1, one launch (start us, length us, event | category | flops | bytes accessed | tf_op | source)
XLA Modules:
  0.0 221.2 jit_solution(16224956101808167653)
XLA Ops:
  6.5 0.0 all-gather.2.cloned.1.call-start
  6.5 0.7 all-gather.2.cloned.1.call-update
  7.3 0.0 all-reduce.2.cloned.1.call-start
  7.3 54.5 %all-gather.2.cloned.1.call-done = bf16[2,1024,1024]{2,1,0:T(8,128)(2,1)} async-done(((bf16[2,64,1024]{2,1,0:T(8,128)(2,1)}), bf16[2,1024,1024]{2,1,0:T(8,128)(2,1)}) %all-gather.2.cloned.1.call-update) | async-done | bytes 4194320 | tf_op jit(solution)/shard_map/all_gather | solution.py:56
  61.8 2.3 %broadcast_select_fusion = bf16[2,1024,1024]{2,1,0:T(8,128)(2,1)} fusion(bf16[2,1024,1024]{2,1,0:T(8,128)(2,1)} %all-gather.2.cloned.1.call-done, pred[]{:T(512)S(6)} %eq.14), kind=kLoop, calls=%fused_computation.30 | loop fusion | flops 2097152 | bytes 8388609 | tf_op jit(solution)/shard_map/jit(_where)/select_n | solution.py:8
  64.1 0.0 copy-start.5
  64.1 0.0 copy-start.3
  64.1 0.0 copy-start.4
  64.1 0.0 copy-start.2
  64.1 0.0 all-reduce.2.cloned.1.call-update
  64.1 0.6 copy-done.5
  64.8 0.1 copy-done.3
  64.8 0.1 reshape.45
  64.9 0.0 copy-done.4
  64.9 0.1 reshape.41
  65.0 0.0 copy-done.2
  65.0 0.0 copy-start
  65.0 2.0 fusion.18
  67.0 2.0 fusion.19
  69.0 2.0 fusion.21
  71.0 2.0 fusion.20
  73.0 0.1 add_divide_fusion
  73.2 0.0 copy-done
  73.2 1.8 slice_bitcast_fusion.3
  75.0 102.2 %all-reduce.2.cloned.1.call-done = bf16[2,1024,1024]{2,1,0:T(8,128)(2,1)} async-done(((bf16[2,1024,1024]{2,1,0:T(8,128)(2,1)}), bf16[2,1024,1024]{2,1,0:T(8,128)(2,1)}) %all-reduce.2.cloned.1.call-update) | async-done | bytes 4194320 | tf_op jit(solution)/shard_map/psum | solution.py:9
  177.2 2.9 %fusion = (bf16[2,1024,1024]{2,1,0:T(8,128)(2,1)S(1)}, bf16[2,1024,1024]{2,1,0:T(8,128)(2,1)S(1)}) fusion(bf16[2,1024,1024]{2,1,0:T(8,128)(2,1)} %all-reduce.2.cloned.1.call-done, f32[1024]{0:T(1024)S(1)} %bitcast.40, f32[1024]{0:T(1024)S(1)} %bitcast.41), kind=kLoop, calls=%fused_computation.3 | loop fusion | flops 10485760 | bytes 12591104 | tf_op jit(solution)/shard_map/convert_element_type | solution.py:41
  180.1 0.3 fusion.42
  180.4 0.0 copy-start.1
  180.4 1.1 slice_bitcast_fusion.1
  181.6 0.4 copy-done.1
  182.0 4.7 %fusion.25 = f32[1,1024,1024]{2,1,0:T(8,128)S(1)} fusion(bf16[1024,1024]{1,0:T(8,128)(2,1)S(1)} %get-tuple-element.10, bf16[1024,1024]{1,0:T(8,128)(2,1)S(1)} %get-tuple-element.9, bf16[1024,1024]{1,0:T(8,128)(2,1)S(1)} %copy-done.1, bf16[1024,1024]{1,0:T(8,128)(2,1)S(1)} %get-tuple-element.11), kind=kOutput, calls=%fused_computation.32 | convolution fusion | flops 4311744512 | bytes 12582912 | tf_op jit(solution)/shard_map/dot_general | solution.py:46
  186.7 4.7 %fusion.22 = f32[1,1024,1024]{2,1,0:T(8,128)S(1)} fusion(bf16[1024,1024]{1,0:T(8,128)(2,1)S(1)} %get-tuple-element.22, bf16[1024,1024]{1,0:T(8,128)(2,1)S(1)} %get-tuple-element.10, bf16[1024,1024]{1,0:T(8,128)(2,1)S(1)} %copy-done.1, bf16[1024,1024]{1,0:T(8,128)(2,1)S(1)} %get-tuple-element.11), kind=kOutput, calls=%fused_computation.31 | convolution fusion | flops 4311744512 | bytes 12582912 | tf_op jit(solution)/shard_map/dot_general | solution.py:49
  191.3 4.9 %fusion.31 = f32[1,1024,1024]{2,1,0:T(8,128)S(1)} fusion(bf16[1024,1024]{1,0:T(8,128)(2,1)S(1)} %get-tuple-element.19, bf16[1024,1024]{1,0:T(8,128)(2,1)S(1)} %get-tuple-element.20, bf16[1024,1024]{1,0:T(8,128)(2,1)S(1)} %copy-done.1, bf16[1024,1024]{1,0:T(8,128)(2,1)S(1)} %get-tuple-element.11), kind=kOutput, calls=%fused_computation.34 | convolution fusion | flops 4311744512 | bytes 12582912 | tf_op jit(solution)/shard_map/dot_general | solution.py:46
  196.3 6.8 %fusion.28 = f32[1,1024,1024]{2,1,0:T(8,128)} fusion(bf16[1024,1024]{1,0:T(8,128)(2,1)S(1)} %get-tuple-element.21, bf16[1024,1024]{1,0:T(8,128)(2,1)S(1)} %get-tuple-element.19, bf16[1024,1024]{1,0:T(8,128)(2,1)S(1)} %copy-done.1, bf16[1024,1024]{1,0:T(8,128)(2,1)S(1)} %get-tuple-element.11), kind=kOutput, calls=%fused_computation.33 | convolution fusion | flops 4311744512 | bytes 12582912 | tf_op jit(solution)/shard_map/dot_general | solution.py:49
  203.0 1.7 maximum_bitcast_fusion.1
  204.7 3.4 %maximum_bitcast_fusion = f32[1,2,1024,1024]{3,2,1,0:T(8,128)S(1)} fusion(f32[1,1024,1024]{2,1,0:T(8,128)} %fusion.28, f32[1,1024,1024]{2,1,0:T(8,128)S(1)} %fusion.31), kind=kLoop, calls=%fused_computation.5 | loop fusion | flops 2097152 | bytes 16777216 | tf_op jit(solution)/shard_map/stack | solution.py:51
  208.1 6.2 %pad_maximum_fusion = f32[2,2,1024,1024]{3,2,1,0:T(8,128)} fusion(f32[1,2,1024,1024]{3,2,1,0:T(8,128)S(1)} %maximum_bitcast_fusion.1, f32[1,2,1024,1024]{3,2,1,0:T(8,128)S(1)} %maximum_bitcast_fusion), kind=kLoop, calls=%fused_computation | loop fusion | flops 4194304 | bytes 33554432 | tf_op jit(solution)/shard_map/stack | solution.py:51
  (5 shorter events, 0.0 us)
Async XLA Ops:
  6.5 55.3 %all-gather.2.cloned.1.call-start = ((), (), s32[]{:S(2)}) async-start(), calls=%async_computation | async-start | bytes 4456448 | tf_op jit(solution)/shard_map/all_gather | solution.py:56
  7.3 169.9 %all-reduce.2.cloned.1.call-start = ((), (), s32[]{:S(2)}) async-start(), calls=%async_computation.1 | async-start | bytes 8388608 | tf_op jit(solution)/shard_map/psum | solution.py:9
  64.1 0.7 copy-start.5
  64.1 0.7 copy-start.3
  64.1 0.8 copy-start.4
  64.1 0.9 copy-start.2
  65.0 8.2 %copy-start = (bf16[2,1024,1024]{2,1,0:T(8,128)(2,1)S(1)}, bf16[2,1024,1024]{2,1,0:T(8,128)(2,1)}, u32[]{:S(2)}) copy-start(bf16[2,1024,1024]{2,1,0:T(8,128)(2,1)} %all-gather.2.cloned.1.call-done) | copy-start | bytes 12582916
  180.4 1.6 copy-start.1
Sparse Core Ops, SparseCore 0:
  9.0 52.7 all-gather.1
  64.3 112.8 all-reduce.1
where the time goes:
time: 221 us
  waiting for transfers between devices  157 us (71%)
  matrix products  29 us (13%)
  other arithmetic  17 us (8%)
  between operations  13.5 us (6%)
  local copies, waits for them, and re-layouts  4.23 us (2%)
    psum x1, waiting for transfers between devices, broadcast(): return lax.psum(kept, axis)  102 us
    all_gather x1, waiting for transfers between devices, body(): lax.all_gather(pair_elements, ('row', 'freq'), axis=1, tiled=True)  54.5 us
    dot_general x2, matrix products, contribute(): lax.dot_general(imag_left, right_both, dims, preferred_element_type=jnp.f...  11.4 us
    another operation x3, other arithmetic, contribute(): return jnp.stack(results, 0)  11.3 us
    dot_general x2, matrix products, contribute(): lax.dot_general(real_left, right_both, dims, preferred_element_type=jnp.f...  9.55 us
    dot_general x4, matrix products, lookup(): return jnp.dot(onehot, flat, precision=lax.Precision.HIGHEST)  8.03 us
  transfers between devices with their start and end apart: 2, of which 2 were waited for; matrix products, arithmetic and copies ran while one was open for 5% of the time, Pallas kernels for 0%

commit v1 on v0

--- a/solution.py
+++ b/solution.py
@@ -6,7 +6,7 @@
 
 def broadcast(value, axis, source):
     kept = jnp.where(lax.axis_index(axis) == source, value, 0).astype(value.dtype)
-    return lax.psum(kept, axis)
+    return jnp.sum(lax.all_gather(kept, axis), axis=0)
 
 
 def lookup(table, flat_rows):

time: 221 us -> 465 us (2.10)
  waiting for transfers between devices: 157 us -> 387 us
  other arithmetic: 17 us -> 31.2 us
    all_gather x0 -> x1, waiting for transfers between devices: none -> 331 us  [broadcast(): return jnp.sum(lax.all_gather(kept, axis), axis=0)]
    psum x1 -> x0, waiting for transfers between devices: 102 us -> none  [broadcast(): return lax.psum(kept, axis)]
    reduce_sum x0 -> x1, other arithmetic: none -> 14.2 us  [broadcast(): return jnp.sum(lax.all_gather(kept, axis), axis=0)]
  transfers between devices with their start and end apart: 2 -> 2, of which waited for: 2 -> 2; matrix products, arithmetic and copies ran while one was open for 5% -> 2% of each run, Pallas kernels for 0% -> 0%
where the time goes in v1:
time: 465 us
  waiting for transfers between devices  387 us (83%)
  other arithmetic  31.2 us (7%)
  matrix products  29 us (6%)
  between operations  13.5 us (3%)
    all_gather x1, waiting for transfers between devices, broadcast(): return jnp.sum(lax.all_gather(kept, axis), axis=0)  331 us
    all_gather x1, waiting for transfers between devices, body(): lax.all_gather(pair_elements, ('row', 'freq'), axis=1, tiled=True)  54.5 us
    reduce_sum x1, other arithmetic, broadcast(): return jnp.sum(lax.all_gather(kept, axis), axis=0)  14.2 us
    dot_general x2, matrix products, contribute(): lax.dot_general(real_left, right_both, dims, preferred_element_type=jnp.f...  11.4 us
    another operation x3, other arithmetic, contribute(): return jnp.stack(results, 0)  11.3 us
    dot_general x2, matrix products, contribute(): lax.dot_general(imag_left, right_both, dims, preferred_element_type=jnp.f...  9.56 us
  transfers between devices with their start and end apart: 2, of which 2 were waited for; matrix products, arithmetic and copies ran while one was open for 2% of the time, Pallas kernels for 0%

profile of v1, /device:TPU:1, one launch (start us, length us, event | category | flops | bytes accessed | tf_op | source)
XLA Modules:
  0.0 464.5 jit_solution(5997450776059891514)
XLA Ops:
  6.5 0.0 all-gather.4.cloned.1.call-start
  6.5 0.7 all-gather.4.cloned.1.call-update
  7.3 0.0 all-gather.6.cloned.1.call-start
  7.3 54.5 %all-gather.4.cloned.1.call-done = bf16[2,1024,1024]{2,1,0:T(8,128)(2,1)} async-done(((bf16[2,64,1024]{2,1,0:T(8,128)(2,1)}), bf16[2,1024,1024]{2,1,0:T(8,128)(2,1)}) %all-gather.4.cloned.1.call-update) | async-done | bytes 4194320 | tf_op jit(solution)/shard_map/all_gather | solution.py:56
  61.8 2.3 broadcast_select_fusion
  64.1 0.0 copy-start.4
  64.1 0.0 copy-start.3
  64.1 0.0 copy-start.5
  64.1 0.0 copy-start.2
  64.1 0.0 all-gather.6.cloned.1.call-update
  64.1 0.7 copy-done.4
  64.8 0.1 reshape.42
  64.9 0.0 copy-done.3
  64.9 0.1 reshape.46
  65.0 0.0 copy-done.5
  65.0 0.0 copy-start
  65.0 0.0 copy-done.2
  65.0 2.0 fusion.21
  67.0 2.0 fusion.19
  69.0 2.0 fusion.18
  71.0 2.0 fusion.20
  73.0 0.1 add_divide_fusion
  73.2 0.0 copy-done
  73.2 1.8 slice_bitcast_fusion.3
  74.9 331.4 %all-gather.6.cloned.1.call-done = bf16[16,1024,1024]{2,1,0:T(8,128)(2,1)} async-done(((bf16[2,1024,1024]{2,1,0:T(8,128)(2,1)}), bf16[16,1024,1024]{2,1,0:T(8,128)(2,1)}) %all-gather.6.cloned.1.call-update) | async-done | bytes 33554448 | tf_op jit(solution)/shard_map/all_gather | solution.py:9
  406.3 14.2 %reduce_sum.12 = bf16[2,1024,1024]{2,1,0:T(8,128)(2,1)} reduce(bf16[8,2,1024,1024]{3,2,1,0:T(8,128)(2,1)} %bitcast.41, bf16[]{:T(256)} %constant.16.clone.1), dimensions={0}, to_apply=%region_0.1 | reduce | flops 14680064 | bytes 37748736 | tf_op jit(solution)/shard_map/reduce_sum | solution.py:9
  420.5 2.9 fusion
  423.5 0.3 fusion.42
  423.7 0.0 copy-start.1
  423.7 1.1 slice_bitcast_fusion.1
  424.9 0.4 copy-done.1
  425.3 4.7 %fusion.22 = f32[1,1024,1024]{2,1,0:T(8,128)S(1)} fusion(bf16[1024,1024]{1,0:T(8,128)(2,1)S(1)} %get-tuple-element.22, bf16[1024,1024]{1,0:T(8,128)(2,1)S(1)} %get-tuple-element.10, bf16[1024,1024]{1,0:T(8,128)(2,1)S(1)} %copy-done.1, bf16[1024,1024]{1,0:T(8,128)(2,1)S(1)} %get-tuple-element.11), kind=kOutput, calls=%fused_computation.31 | convolution fusion | flops 4311744512 | bytes 12582912 | tf_op jit(solution)/shard_map/dot_general | solution.py:49
  430.0 4.7 %fusion.25 = f32[1,1024,1024]{2,1,0:T(8,128)S(1)} fusion(bf16[1024,1024]{1,0:T(8,128)(2,1)S(1)} %get-tuple-element.10, bf16[1024,1024]{1,0:T(8,128)(2,1)S(1)} %get-tuple-element.9, bf16[1024,1024]{1,0:T(8,128)(2,1)S(1)} %copy-done.1, bf16[1024,1024]{1,0:T(8,128)(2,1)S(1)} %get-tuple-element.11), kind=kOutput, calls=%fused_computation.32 | convolution fusion | flops 4311744512 | bytes 12582912 | tf_op jit(solution)/shard_map/dot_general | solution.py:46
  434.7 4.9 %fusion.28 = f32[1,1024,1024]{2,1,0:T(8,128)S(1)} fusion(bf16[1024,1024]{1,0:T(8,128)(2,1)S(1)} %get-tuple-element.21, bf16[1024,1024]{1,0:T(8,128)(2,1)S(1)} %get-tuple-element.19, bf16[1024,1024]{1,0:T(8,128)(2,1)S(1)} %copy-done.1, bf16[1024,1024]{1,0:T(8,128)(2,1)S(1)} %get-tuple-element.11), kind=kOutput, calls=%fused_computation.33 | convolution fusion | flops 4311744512 | bytes 12582912 | tf_op jit(solution)/shard_map/dot_general | solution.py:49
  439.6 6.8 %fusion.31 = f32[1,1024,1024]{2,1,0:T(8,128)} fusion(bf16[1024,1024]{1,0:T(8,128)(2,1)S(1)} %get-tuple-element.19, bf16[1024,1024]{1,0:T(8,128)(2,1)S(1)} %get-tuple-element.20, bf16[1024,1024]{1,0:T(8,128)(2,1)S(1)} %copy-done.1, bf16[1024,1024]{1,0:T(8,128)(2,1)S(1)} %get-tuple-element.11), kind=kOutput, calls=%fused_computation.34 | convolution fusion | flops 4311744512 | bytes 12582912 | tf_op jit(solution)/shard_map/dot_general | solution.py:46
  446.3 1.7 maximum_bitcast_fusion.1
  448.0 3.4 maximum_bitcast_fusion
  451.4 6.2 %pad_maximum_fusion = f32[2,2,1024,1024]{3,2,1,0:T(8,128)} fusion(f32[1,2,1024,1024]{3,2,1,0:T(8,128)S(1)} %maximum_bitcast_fusion.1, f32[1,2,1024,1024]{3,2,1,0:T(8,128)S(1)} %maximum_bitcast_fusion), kind=kLoop, calls=%fused_computation | loop fusion | flops 4194304 | bytes 33554432 | tf_op jit(solution)/shard_map/stack | solution.py:51
  (5 shorter events, 0.0 us)
Async XLA Ops:
  6.5 55.3 %all-gather.4.cloned.1.call-start = ((), (), s32[]{:S(2)}) async-start(), calls=%async_computation | async-start | bytes 4456448 | tf_op jit(solution)/shard_map/all_gather | solution.py:56
  7.3 399.0 %all-gather.6.cloned.1.call-start = ((), (), s32[]{:S(2)}) async-start(), calls=%async_computation.1 | async-start | bytes 37748736 | tf_op jit(solution)/shard_map/all_gather | solution.py:9
  64.1 0.7 copy-start.4
  64.1 0.8 copy-start.3
  64.1 0.9 copy-start.5
  64.1 0.9 copy-start.2
  65.0 8.2 %copy-start = (bf16[2,1024,1024]{2,1,0:T(8,128)(2,1)S(1)}, bf16[2,1024,1024]{2,1,0:T(8,128)(2,1)}, u32[]{:S(2)}) copy-start(bf16[2,1024,1024]{2,1,0:T(8,128)(2,1)} %all-gather.4.cloned.1.call-done) | copy-start | bytes 12582916
  423.7 1.6 copy-start.1
Sparse Core Ops, SparseCore 0:
  9.0 52.7 all-gather.3
  64.3 341.9 all-gather.5
